TPU v7x, 256 devices: a whole 4x4x8 slice. The times are simulated.
256 devices in a mesh: gx: 32 (over z, x), gy: 8 (over y, core).
Axes of the slice: x: 4, y: 4, z: 8, core: 2. Of those that a mesh axis runs over, the one named last changes fastest.
Arguments:
- right_side: float32 [8192, 512], P(('gx', 'gy')), may hold values from -6 to 6
- diagonal: float32 [8192, 512], P(('gx', 'gy')), may hold values from 0.5 to 2
- features: float32 [8192, 64, 512], P(('gx', 'gy')), may hold values from -0.078125 to 0.078125
- neighbours: int32 [8192, 27], P(('gx', 'gy')), may hold values from -1 to 8191, as said below
- vertex_features: float32 [64, 262144], P(None, ('gx', 'gy')), may hold values from -0.75 to 0.75
- vertex_bricks: int32 [262144], P(('gx', 'gy')), may hold values from 0 to 8191, as said below
Outputs:
- solution_field: float32 [8192, 512], P(('gx', 'gy'))
- residual: float32 [8192, 512], P(('gx', 'gy'))
- vertex_values: float32 [262144], P(('gx', 'gy'))
Inputs may be any that keep to these rules, and one draw needn't show every extreme that they name: `neighbours`: bricks sit at distinct integer brick coordinates; slot k of a row names the brick at the offset (k // 9 - 1, k // 3 % 3 - 1, k % 3 - 1) from its own, or -1 where no brick is there, so slot 13 names the brick itself and the relation is symmetric. Every brick whose coordinates differ from a brick's by at most two in each direction is held by a device whose gx and gy indices each differ from that brick's holder's by at most one. `vertex_bricks`: vertex n names a brick of its own gx slab: a brick from (n // 8192) * 256 to (n // 8192) * 256 + 255.
All inputs are finite; a program needn't handle non-finite values.
Results may differ from a plain program's by a relative error of at most 0.0002.
Values sent between devices are 32-bit elements; how exact they have to be, the bound alone decides.
No kernel may reach another device: no remote copies, remote signals or barrier semaphores. Data moves between devices by JAX's collectives and lax.ppermute only.
A program may use at most 64 MiB of HBM per device.

v0:
```python
import jax
import jax.numpy as jnp
from jax import lax
from jax.sharding import PartitionSpec as P

ITERS = 3


def with_halo(cells, sides, width):
    for axis, dim in sides:
        count = lax.axis_size(axis)
        ends = count - 1
        head = lax.slice_in_dim(cells, 0, width, axis=dim)
        tail = lax.slice_in_dim(cells, cells.shape[dim] - width, cells.shape[dim], axis=dim)
        cells = jnp.concatenate(
            [
                lax.ppermute(tail, axis, [(i, (i + 1) % count) for i in range(ends)]),
                cells,
                lax.ppermute(head, axis, [((i + 1) % count, i) for i in range(ends)]),
            ],
            axis=dim,
        )
    return cells


def coefficient(features, field):
    return jnp.einsum("bfv,bv->bf", features, field, precision=lax.Precision.HIGHEST)


def squares(values):
    return lax.psum(jnp.sum(values * values), ("gx", "gy"))


def per_device(right_side, diagonal, features, neighbours, vertex_features, vertex_bricks):
    nrows = features.shape[0]
    width = features.shape[1]
    across = lax.axis_size("gy")
    row_index = lax.axis_index("gx")
    col_index = lax.axis_index("gy")
    targets = jnp.arange(9 * nrows, dtype=jnp.int32)
    valid = neighbours >= 0
    safe_ids = jnp.where(valid, neighbours, 0)
    owner = safe_ids // nrows
    offset_x = owner // across - row_index + 1
    offset_y = owner % across - col_index + 1
    inside = valid & (offset_x >= 0) & (offset_x < 3) & (offset_y >= 0) & (offset_y < 3)
    position, inside = ((offset_x * 3 + offset_y) * nrows + safe_ids % nrows, inside)
    hits = (position[:, :, None] == targets[None, None, :]) & inside[:, :, None]
    counts = jnp.sum(hits.astype(jnp.float32), axis=1)

    def first_halo(values):
        cycle = with_halo(values.reshape(1, 1, nrows, width), (("gx", 0), ("gy", 1)), 1)
        return cycle.reshape(9 * nrows, width)

    def first_sum(values):
        return jnp.dot(counts, first_halo(values), precision=lax.Precision.HIGHEST)

    solution_field = jnp.zeros_like(right_side)
    residual = right_side
    direction = right_side
    norm_now = squares(residual)
    for step in range(ITERS):
        second_cycle = with_halo(
            first_sum(coefficient(features, direction)).reshape(1, 1, nrows, width),
            (("gx", 0), ("gy", 1)),
            1,
        )
        second = jnp.dot(
            counts, second_cycle.reshape(9 * nrows, width), precision=lax.Precision.HIGHEST
        )
        image = diagonal * direction + jnp.einsum(
            "bfv,bf->bv", features, second, precision=lax.Precision.HIGHEST
        )
        alpha = norm_now / lax.psum(jnp.sum(direction * image), ("gx", "gy"))
        solution_field = solution_field + alpha * direction
        residual = residual - alpha * image
        norm_next = squares(residual)
        direction = residual + norm_next / norm_now * direction
        norm_now = norm_next
    surface = first_sum(coefficient(features, solution_field))
    slab_rows = lax.all_gather(surface, "gy", axis=0, tiled=True)
    local_ids = vertex_bricks - row_index * across * nrows
    picked = jnp.take(slab_rows, local_ids, axis=0)
    vertex_values = jnp.sum(vertex_features * picked.T, axis=0)
    return (solution_field, residual, vertex_values)


def solution(mesh):
    placed = (
        P(("gx", "gy"), None),
        P(("gx", "gy"), None),
        P(("gx", "gy"), None, None),
        P(("gx", "gy"), None),
        P(None, ("gx", "gy")),
        P(("gx", "gy")),
    )
    return jax.shard_map(
        per_device,
        mesh=mesh,
        in_specs=placed,
        out_specs=(P(("gx", "gy"), None), P(("gx", "gy"), None), P(("gx", "gy"))),
        check_vma=False,
    )
```

profile of v0, /device:TPU:129, one launch (start us, length us, event | category | flops | bytes accessed | tf_op | source)
XLA Modules:
  0.0 560.7 jit_solution(662496368784365687)
XLA Ops:
  0.7 5.8 %fusion.8 = f32[32,1,64]{2,1,0:T(1,128)S(1)} fusion(f32[32,64,512]{2,1,0:T(8,128)} %param.8, f32[32,512,1]{1,0,2:T(8,128)} %bitcast.92), kind=kOutput, calls=%fused_computation.25 | convolution fusion | flops 12582912 | bytes 4268032 | tf_op jit(solution)/shard_map/bfv,bv->bf/dot_general | solution.py:27
  6.5 3.9 collective-permute-start.1
  10.4 1.9 collective-permute-start
  12.7 5.6 collective-permute-done
  18.2 4.0 collective-permute-start.3
  22.3 3.1 collective-permute-start.2
  25.4 0.3 convert_reduce_fusion
  25.7 0.8 collective-permute-done.2
  26.8 1.9 collective-permute-start.5
  28.7 3.4 collective-permute-start.4
  32.1 4.4 collective-permute-done.4
  36.5 2.1 collective-permute-start.7
  38.6 5.2 collective-permute-start.6
  43.8 1.1 collective-permute-done.6
  45.2 4.3 fusion.25
  49.5 0.6 multiply_reduce_fusion.4
  50.2 74.5 %all-reduce = (f32[]{:T(128)}, f32[]{:T(128)}) all-reduce(f32[]{:T(128)} %get-tuple-element.4, f32[]{:T(128)} %get-tuple-element.3), channel_id=1, replica_groups=mesh['gx'=32,'gy'=8] {'gx','gy'}, use_global_device_ids=true, to_apply=%region_1.2 | all-reduce | flops 2 | bytes 16 | tf_op jit(solution)/shard_map/psum | solution.py:31
  126.0 0.6 multiply_reduce_fusion.3
  126.7 73.5 %psum.44 = f32[]{:T(128)} all-reduce(f32[]{:T(128)} %get-tuple-element.9), channel_id=1, replica_groups=mesh['gx'=32,'gy'=8] {'gx','gy'}, use_global_device_ids=true, to_apply=%region_6.7 | all-reduce | flops 1 | bytes 8 | tf_op jit(solution)/shard_map/psum | solution.py:31
  201.5 5.4 fusion.6
  206.9 3.8 collective-permute-start.9
  210.8 1.9 collective-permute-start.8
  212.7 5.9 %collective-permute-done.8 = f32[1,1,32,64]{3,2,1,0:T(8,128)S(1)} collective-permute-done((f32[1,1,32,64]{3,2,1,0:T(8,128)S(1)}, f32[1,1,32,64]{3,2,1,0:T(8,128)S(1)}, u32[]{:S(2)}, u32[]{:S(2)}) %collective-permute-start.8) | collective-permute-done | bytes 8224 | tf_op jit(solution)/shard_map/ppermute | solution.py:17
  218.6 4.0 collective-permute-start.11
  222.6 1.9 collective-permute-start.10
  224.5 1.2 collective-permute-done.10
  226.0 1.9 collective-permute-start.13
  227.9 3.4 collective-permute-start.12
  231.3 4.4 collective-permute-done.12
  235.7 3.2 collective-permute-start.15
  238.9 4.3 collective-permute-start.14
  243.2 1.0 collective-permute-done.14
  244.4 2.1 fusion.27
  246.5 0.6 multiply_reduce_fusion.2
  247.1 73.2 %psum.45 = f32[]{:T(128)} all-reduce(f32[]{:T(128)} %multiply_reduce_fusion.2), channel_id=1, replica_groups=mesh['gx'=32,'gy'=8] {'gx','gy'}, use_global_device_ids=true, to_apply=%region_8.9 | all-reduce | flops 1 | bytes 8 | tf_op jit(solution)/shard_map/psum | solution.py:74
  321.7 0.6 multiply_reduce_fusion.1
  322.3 73.3 %psum.46 = f32[]{:T(128)} all-reduce(f32[]{:T(128)} %get-tuple-element.7), channel_id=1, replica_groups=mesh['gx'=32,'gy'=8] {'gx','gy'}, use_global_device_ids=true, to_apply=%region_10.11 | all-reduce | flops 1 | bytes 8 | tf_op jit(solution)/shard_map/psum | solution.py:31
  397.0 5.4 fusion.4
  402.4 4.2 collective-permute-start.17
  406.6 1.9 collective-permute-start.16
  408.6 5.9 %collective-permute-done.16 = f32[1,1,32,64]{3,2,1,0:T(8,128)S(1)} collective-permute-done((f32[1,1,32,64]{3,2,1,0:T(8,128)S(1)}, f32[1,1,32,64]{3,2,1,0:T(8,128)S(1)}, u32[]{:S(2)}, u32[]{:S(2)}) %collective-permute-start.16) | collective-permute-done | bytes 8224 | tf_op jit(solution)/shard_map/ppermute | solution.py:17
  414.5 4.0 collective-permute-start.19
  418.5 1.9 collective-permute-start.18
  420.4 1.2 collective-permute-done.18
  421.8 1.9 collective-permute-start.21
  423.7 3.4 collective-permute-start.20
  427.1 4.4 collective-permute-done.20
  431.6 3.2 collective-permute-start.23
  434.8 4.1 collective-permute-start.22
  438.9 1.1 collective-permute-done.22
  440.3 2.1 fusion.29
  442.4 0.6 multiply_reduce_fusion
  443.0 73.2 %psum.47 = f32[]{:T(128)} all-reduce(f32[]{:T(128)} %multiply_reduce_fusion), channel_id=1, replica_groups=mesh['gx'=32,'gy'=8] {'gx','gy'}, use_global_device_ids=true, to_apply=%region_12.13 | all-reduce | flops 1 | bytes 8 | tf_op jit(solution)/shard_map/psum | solution.py:74
  517.5 0.7 multiply_subtract_fusion
  518.2 5.3 fusion.2
  523.5 3.7 collective-permute-start.25
  527.2 1.9 collective-permute-start.24
  529.2 5.8 %collective-permute-done.24 = f32[1,1,32,64]{3,2,1,0:T(8,128)S(1)} collective-permute-done((f32[1,1,32,64]{3,2,1,0:T(8,128)S(1)}, f32[1,1,32,64]{3,2,1,0:T(8,128)S(1)}, u32[]{:S(2)}, u32[]{:S(2)}) %collective-permute-start.24) | collective-permute-done | bytes 8224 | tf_op jit(solution)/shard_map/ppermute | solution.py:17
  535.0 4.0 collective-permute-start.27
  539.0 3.4 collective-permute-start.26
  542.7 0.9 collective-permute-done.26
  543.8 13.1 %all_gather.3 = f32[256,64]{1,0:T(8,128)S(1)} all-gather(f32[32,64]{1,0:T(8,128)S(1)} %fusion.30), channel_id=1, replica_groups=mesh['gx'=32,'gy'=8] {'gy'}, dimensions={0}, use_global_device_ids=true | all-gather | bytes 73728 | tf_op jit(solution)/shard_map/all_gather | solution.py:81
  556.9 2.8 gather_fusion
  559.7 1.0 fusion.1
  (60 shorter events, 2.2 us)
Async XLA Ops:
  0.6 11.7 %copy-start.6 = (s32[32,27]{1,0:T(8,128)S(1)}, s32[32,27]{1,0:T(8,128)}, u32[]{:S(2)}) copy-start(s32[32,27]{1,0:T(8,128)} %param.9) | copy-start | bytes 10372
  0.6 48.9 %copy-start.2 = (f32[32,512]{1,0:T(8,128)S(1)}, f32[32,512]{1,0:T(8,128)}, u32[]{:S(2)}) copy-start(f32[32,512]{1,0:T(8,128)} %param.7) | copy-start | bytes 196612
  0.7 48.9 %copy-start.3 = (f32[32,512]{1,0:T(8,128)S(1)}, f32[32,512]{1,0:T(8,128)}, u32[]{:S(2)}) copy-start(f32[32,512]{1,0:T(8,128)} %param.6) | copy-start | bytes 196612
  6.5 6.2 %collective-permute-start.1 = (f32[1,1,32,64]{3,2,1,0:T(8,128)S(1)}, f32[1,1,32,64]{3,2,1,0:T(8,128)S(1)}, u32[]{:S(2)}, u32[]{:S(2)}) collective-permute-start(f32[1,1,32,64]{3,2,1,0:T(8,128)S(1)} %bitcast.101), channel_id=1, source_target_pairs={{8,0},{16,8},{24,16},{32,24},{40,32},{48,40},{56,48},{64,56},{72,6... | collective-permute-start | bytes 24584 | tf_op jit(solution)/shard_map/ppermute | solution.py:19
  10.4 7.8 %collective-permute-start = (f32[1,1,32,64]{3,2,1,0:T(8,128)S(1)}, f32[1,1,32,64]{3,2,1,0:T(8,128)S(1)}, u32[]{:S(2)}, u32[]{:S(2)}) collective-permute-start(f32[1,1,32,64]{3,2,1,0:T(8,128)S(1)} %bitcast.102), channel_id=1, source_target_pairs={{0,8},{8,16},{16,24},{24,32},{32,40},{40,48},{48,56},{56,64},{64,7... | collective-permute-start | bytes 24584 | tf_op jit(solution)/shard_map/ppermute | solution.py:17
  18.2 7.4 %collective-permute-start.3 = (f32[3,1,32,64]{3,2,1,0:T(8,128)S(1)}, f32[3,1,32,64]{3,2,1,0:T(8,128)S(1)}, u32[]{:S(2)}, u32[]{:S(2)}) collective-permute-start(f32[3,1,32,64]{3,2,1,0:T(8,128)S(1)} %pad_maximum_fusion.7), channel_id=1, source_target_pairs={{1,0},{2,1},{3,2},{4,3},{5,4},{6,5},{7,6},{9,8},{10,9},{11,10},{12... | collective-permute-start | bytes 73736 | tf_op jit(solution)/shard_map/ppermute | solution.py:19
  22.3 4.3 collective-permute-start.2
  26.8 5.3 collective-permute-start.5
  28.7 7.8 %collective-permute-start.4 = (f32[1,1,32,64]{3,2,1,0:T(8,128)S(1)}, f32[1,1,32,64]{3,2,1,0:T(8,128)S(1)}, u32[]{:S(2)}, u32[]{:S(2)}) collective-permute-start(f32[1,1,32,64]{3,2,1,0:T(8,128)S(1)} %convolution_bitcast_fusion.2), channel_id=1, source_target_pairs={{0,8},{8,16},{16,24},{24,32},{32,40},{40,48},{48,56},{56,64},{64,7... | collective-permute-start | bytes 24584 | tf_op jit(solution)/shard_map/ppermute | solution.py:17
  36.5 7.3 %collective-permute-start.7 = (f32[3,1,32,64]{3,2,1,0:T(8,128)S(1)}, f32[3,1,32,64]{3,2,1,0:T(8,128)S(1)}, u32[]{:S(2)}, u32[]{:S(2)}) collective-permute-start(f32[3,1,32,64]{3,2,1,0:T(8,128)S(1)} %pad_maximum_fusion.8), channel_id=1, source_target_pairs={{1,0},{2,1},{3,2},{4,3},{5,4},{6,5},{7,6},{9,8},{10,9},{11,10},{12... | collective-permute-start | bytes 73736 | tf_op jit(solution)/shard_map/ppermute | solution.py:19
  38.6 6.4 %collective-permute-start.6 = (f32[3,1,32,64]{3,2,1,0:T(8,128)S(1)}, f32[3,1,32,64]{3,2,1,0:T(8,128)S(1)}, u32[]{:S(2)}, u32[]{:S(2)}) collective-permute-start(f32[3,1,32,64]{3,2,1,0:T(8,128)S(1)} %pad_maximum_fusion.8), channel_id=1, source_target_pairs={{0,1},{1,2},{2,3},{3,4},{4,5},{5,6},{6,7},{8,9},{9,10},{10,11},{11... | collective-permute-start | bytes 73736 | tf_op jit(solution)/shard_map/ppermute | solution.py:17
  201.5 42.9 %copy-start = (f32[32,64,512]{2,1,0:T(8,128)S(1)}, f32[32,64,512]{2,1,0:T(8,128)}, u32[]{:S(2)}) copy-start(f32[32,64,512]{2,1,0:T(8,128)} %param.8) | copy-start | bytes 12582916
  206.9 5.8 %collective-permute-start.9 = (f32[1,1,32,64]{3,2,1,0:T(8,128)S(1)}, f32[1,1,32,64]{3,2,1,0:T(8,128)S(1)}, u32[]{:S(2)}, u32[]{:S(2)}) collective-permute-start(f32[1,1,32,64]{3,2,1,0:T(8,128)S(1)} %bitcast.113), channel_id=1, source_target_pairs={{8,0},{16,8},{24,16},{32,24},{40,32},{48,40},{56,48},{64,56},{72,6... | collective-permute-start | bytes 24584 | tf_op jit(solution)/shard_map/ppermute | solution.py:19
  210.8 7.8 %collective-permute-start.8 = (f32[1,1,32,64]{3,2,1,0:T(8,128)S(1)}, f32[1,1,32,64]{3,2,1,0:T(8,128)S(1)}, u32[]{:S(2)}, u32[]{:S(2)}) collective-permute-start(f32[1,1,32,64]{3,2,1,0:T(8,128)S(1)} %bitcast.114), channel_id=1, source_target_pairs={{0,8},{8,16},{16,24},{24,32},{32,40},{40,48},{48,56},{56,64},{64,7... | collective-permute-start | bytes 24584 | tf_op jit(solution)/shard_map/ppermute | solution.py:17
  218.6 5.9 %collective-permute-start.11 = (f32[3,1,32,64]{3,2,1,0:T(8,128)S(1)}, f32[3,1,32,64]{3,2,1,0:T(8,128)S(1)}, u32[]{:S(2)}, u32[]{:S(2)}) collective-permute-start(f32[3,1,32,64]{3,2,1,0:T(8,128)S(1)} %pad_maximum_fusion.9), channel_id=1, source_target_pairs={{1,0},{2,1},{3,2},{4,3},{5,4},{6,5},{7,6},{9,8},{10,9},{11,10},{12... | collective-permute-start | bytes 73736 | tf_op jit(solution)/shard_map/ppermute | solution.py:19
  222.6 3.1 collective-permute-start.10
  226.0 5.3 collective-permute-start.13
  227.9 7.8 %collective-permute-start.12 = (f32[1,1,32,64]{3,2,1,0:T(8,128)S(1)}, f32[1,1,32,64]{3,2,1,0:T(8,128)S(1)}, u32[]{:S(2)}, u32[]{:S(2)}) collective-permute-start(f32[1,1,32,64]{3,2,1,0:T(8,128)S(1)} %convolution_bitcast_fusion.1), channel_id=1, source_target_pairs={{0,8},{8,16},{16,24},{24,32},{32,40},{40,48},{48,56},{56,64},{64,7... | collective-permute-start | bytes 24584 | tf_op jit(solution)/shard_map/ppermute | solution.py:17
  235.7 7.5 %collective-permute-start.15 = (f32[3,1,32,64]{3,2,1,0:T(8,128)S(1)}, f32[3,1,32,64]{3,2,1,0:T(8,128)S(1)}, u32[]{:S(2)}, u32[]{:S(2)}) collective-permute-start(f32[3,1,32,64]{3,2,1,0:T(8,128)S(1)} %pad_maximum_fusion.10), channel_id=1, source_target_pairs={{1,0},{2,1},{3,2},{4,3},{5,4},{6,5},{7,6},{9,8},{10,9},{11,10},{12... | collective-permute-start | bytes 73736 | tf_op jit(solution)/shard_map/ppermute | solution.py:19
  238.9 5.2 collective-permute-start.14
  396.9 43.3 %copy-start.1 = (f32[32,64,512]{2,1,0:T(8,128)S(1)}, f32[32,64,512]{2,1,0:T(8,128)}, u32[]{:S(2)}) copy-start(f32[32,64,512]{2,1,0:T(8,128)} %param.8) | copy-start | bytes 12582916
  402.4 6.2 %collective-permute-start.17 = (f32[1,1,32,64]{3,2,1,0:T(8,128)S(1)}, f32[1,1,32,64]{3,2,1,0:T(8,128)S(1)}, u32[]{:S(2)}, u32[]{:S(2)}) collective-permute-start(f32[1,1,32,64]{3,2,1,0:T(8,128)S(1)} %bitcast.109), channel_id=1, source_target_pairs={{8,0},{16,8},{24,16},{32,24},{40,32},{48,40},{56,48},{64,56},{72,6... | collective-permute-start | bytes 24584 | tf_op jit(solution)/shard_map/ppermute | solution.py:19
  406.6 7.8 %collective-permute-start.16 = (f32[1,1,32,64]{3,2,1,0:T(8,128)S(1)}, f32[1,1,32,64]{3,2,1,0:T(8,128)S(1)}, u32[]{:S(2)}, u32[]{:S(2)}) collective-permute-start(f32[1,1,32,64]{3,2,1,0:T(8,128)S(1)} %bitcast.110), channel_id=1, source_target_pairs={{0,8},{8,16},{16,24},{24,32},{32,40},{40,48},{48,56},{56,64},{64,7... | collective-permute-start | bytes 24584 | tf_op jit(solution)/shard_map/ppermute | solution.py:17
  414.5 5.9 %collective-permute-start.19 = (f32[3,1,32,64]{3,2,1,0:T(8,128)S(1)}, f32[3,1,32,64]{3,2,1,0:T(8,128)S(1)}, u32[]{:S(2)}, u32[]{:S(2)}) collective-permute-start(f32[3,1,32,64]{3,2,1,0:T(8,128)S(1)} %pad_maximum_fusion.11), channel_id=1, source_target_pairs={{1,0},{2,1},{3,2},{4,3},{5,4},{6,5},{7,6},{9,8},{10,9},{11,10},{12... | collective-permute-start | bytes 73736 | tf_op jit(solution)/shard_map/ppermute | solution.py:19
  418.5 3.1 collective-permute-start.18
  421.8 5.3 collective-permute-start.21
  423.7 7.8 %collective-permute-start.20 = (f32[1,1,32,64]{3,2,1,0:T(8,128)S(1)}, f32[1,1,32,64]{3,2,1,0:T(8,128)S(1)}, u32[]{:S(2)}, u32[]{:S(2)}) collective-permute-start(f32[1,1,32,64]{3,2,1,0:T(8,128)S(1)} %convolution_bitcast_fusion), channel_id=1, source_target_pairs={{0,8},{8,16},{16,24},{24,32},{32,40},{40,48},{48,56},{56,64},{64,7... | collective-permute-start | bytes 24584 | tf_op jit(solution)/shard_map/ppermute | solution.py:17
  431.6 7.3 %collective-permute-start.23 = (f32[3,1,32,64]{3,2,1,0:T(8,128)S(1)}, f32[3,1,32,64]{3,2,1,0:T(8,128)S(1)}, u32[]{:S(2)}, u32[]{:S(2)}) collective-permute-start(f32[3,1,32,64]{3,2,1,0:T(8,128)S(1)} %pad_maximum_fusion.12), channel_id=1, source_target_pairs={{1,0},{2,1},{3,2},{4,3},{5,4},{6,5},{7,6},{9,8},{10,9},{11,10},{12... | collective-permute-start | bytes 73736 | tf_op jit(solution)/shard_map/ppermute | solution.py:19
  434.8 5.2 collective-permute-start.22
  440.2 88.9 %copy-start.7 = (s32[1024]{0:T(1024)S(1)}, s32[1024]{0:T(1024)}, u32[]{:S(2)}) copy-start(s32[1024]{0:T(1024)} %param.11) | copy-start | bytes 12292
  440.3 102.2 %copy-start.5 = (f32[64,1024]{1,0:T(8,128)S(1)}, f32[64,1024]{1,0:T(8,128)}, u32[]{:S(2)}) copy-start(f32[64,1024]{1,0:T(8,128)} %param.10) | copy-start | bytes 786436
  518.2 41.5 %copy-start.4 = (f32[32,512]{1,0:T(8,128)}, f32[32,512]{1,0:T(8,128)S(1)}, u32[]{:S(2)}) copy-start(f32[32,512]{1,0:T(8,128)S(1)} %get-tuple-element.12) | copy-start | bytes 196612
  523.5 5.6 %collective-permute-start.25 = (f32[1,1,32,64]{3,2,1,0:T(8,128)S(1)}, f32[1,1,32,64]{3,2,1,0:T(8,128)S(1)}, u32[]{:S(2)}, u32[]{:S(2)}) collective-permute-start(f32[1,1,32,64]{3,2,1,0:T(8,128)S(1)} %bitcast.105), channel_id=1, source_target_pairs={{8,0},{16,8},{24,16},{32,24},{40,32},{48,40},{56,48},{64,56},{72,6... | collective-permute-start | bytes 24584 | tf_op jit(solution)/shard_map/ppermute | solution.py:19
  527.2 7.8 %collective-permute-start.24 = (f32[1,1,32,64]{3,2,1,0:T(8,128)S(1)}, f32[1,1,32,64]{3,2,1,0:T(8,128)S(1)}, u32[]{:S(2)}, u32[]{:S(2)}) collective-permute-start(f32[1,1,32,64]{3,2,1,0:T(8,128)S(1)} %bitcast.106), channel_id=1, source_target_pairs={{0,8},{8,16},{16,24},{24,32},{32,40},{40,48},{48,56},{56,64},{64,7... | collective-permute-start | bytes 24584 | tf_op jit(solution)/shard_map/ppermute | solution.py:17
  535.0 7.7 %collective-permute-start.27 = (f32[3,1,32,64]{3,2,1,0:T(8,128)S(1)}, f32[3,1,32,64]{3,2,1,0:T(8,128)S(1)}, u32[]{:S(2)}, u32[]{:S(2)}) collective-permute-start(f32[3,1,32,64]{3,2,1,0:T(8,128)S(1)} %pad_maximum_fusion.13), channel_id=1, source_target_pairs={{1,0},{2,1},{3,2},{4,3},{5,4},{6,5},{7,6},{9,8},{10,9},{11,10},{12... | collective-permute-start | bytes 73736 | tf_op jit(solution)/shard_map/ppermute | solution.py:19
  539.0 4.6 collective-permute-start.26
where the time goes:
time: 563 us; the launch traced here: 561 us
  blocking collectives  381 us (68%)
  starting transfers between devices  87.6 us (16%)
  waiting for transfers between devices  43.8 us (8%)
  matrix products  32 us (6%)
  between operations  7.94 us (1%)
    psum x3, blocking collectives, squares(): return lax.psum(jnp.sum(values * values), ('gx', 'gy'))  221 us
    psum x2, blocking collectives, per_device(): alpha = norm_now / lax.psum(jnp.sum(direction * image), ('gx', 'gy'))  146 us
    ppermute x14, starting transfers between devices, with_halo(): lax.ppermute(head, axis, [((i + 1) % count, i) for i in range(ends)])  45.9 us
    ppermute x14, waiting for transfers between devices, with_halo(): lax.ppermute(tail, axis, [(i, (i + 1) % count) for i in range(ends)])  43.8 us
    ppermute x14, starting transfers between devices, with_halo(): lax.ppermute(tail, axis, [(i, (i + 1) % count) for i in range(ends)])  41.7 us
    dot_general x4, matrix products, coefficient(): jnp.einsum('bfv,bv->bf', features, field, precision=lax.Precision.HIGHEST)  22 us
    all_gather x1, blocking collectives, per_device(): slab_rows = lax.all_gather(surface, 'gy', axis=0, tiled=True)  13.1 us
  transfers between devices with their start and end apart: 28, of which 14 were waited for; matrix products, arithmetic and copies ran while one was open for 0% of the time, Pallas kernels for 0%

commit v1 on v0

--- a/solution.py
+++ b/solution.py
@@ -4,6 +4,17 @@
 from jax.sharding import PartitionSpec as P
 
 ITERS = 3
+
+
+def around_the_ring(shard, axis, dim):
+    size = lax.axis_size(axis)
+    right = [(i, (i + 1) % size) for i in range(size)]
+    pieces = [shard]
+    for far in range(1, size):
+        pieces = [lax.ppermute(pieces[0], axis, right), *pieces]
+    whole = jnp.concatenate(pieces, axis=dim)
+    places = (lax.axis_index(axis) + 1) * pieces[-1].shape[dim]
+    return jnp.roll(whole, places, axis=dim)
 
 
 def with_halo(cells, sides, width):
@@ -78,7 +89,7 @@
         direction = residual + norm_next / norm_now * direction
         norm_now = norm_next
     surface = first_sum(coefficient(features, solution_field))
-    slab_rows = lax.all_gather(surface, "gy", axis=0, tiled=True)
+    slab_rows = around_the_ring(surface, "gy", 0)
     local_ids = vertex_bricks - row_index * across * nrows
     picked = jnp.take(slab_rows, local_ids, axis=0)
     vertex_values = jnp.sum(vertex_features * picked.T, axis=0)

time: 563 us -> 579 us (1.028)
  starting transfers between devices: 87.6 us -> 101 us
  blocking collectives: 381 us -> 368 us
  waiting for transfers between devices: 43.8 us -> 56.5 us
    all_gather x1 -> x0, blocking collectives: 13.1 us -> none  [per_device(): slab_rows = lax.all_gather(surface, 'gy', axis=0, tiled=True)]
    ppermute x0 -> x7, starting transfers between devices: none -> 12.9 us  [around_the_ring(): pieces = [lax.ppermute(pieces[0], axis, right), *pieces]]
    ppermute x0 -> x7, waiting for transfers between devices: none -> 12.5 us  [around_the_ring(): pieces = [lax.ppermute(pieces[0], axis, right), *pieces]]
  transfers between devices with their start and end apart: 28 -> 35, of which waited for: 14 -> 21; matrix products, arithmetic and copies ran while one was open for 0% -> 0% of each run, Pallas kernels for 0% -> 0%
where the time goes in v1:
time: 579 us; the launch traced here: 573 us
  blocking collectives  368 us (64%)
  starting transfers between devices  101 us (17%)
  waiting for transfers between devices  56.5 us (10%)
  matrix products  32 us (6%)
  between operations  8.05 us (1%)
    psum x3, blocking collectives, squares(): return lax.psum(jnp.sum(values * values), ('gx', 'gy'))  221 us
    psum x2, blocking collectives, per_device(): alpha = norm_now / lax.psum(jnp.sum(direction * image), ('gx', 'gy'))  146 us
    ppermute x14, starting transfers between devices, with_halo(): lax.ppermute(head, axis, [((i + 1) % count, i) for i in range(ends)])  45.9 us
    ppermute x14, waiting for transfers between devices, with_halo(): lax.ppermute(tail, axis, [(i, (i + 1) % count) for i in range(ends)])  44 us
    ppermute x14, starting transfers between devices, with_halo(): lax.ppermute(tail, axis, [(i, (i + 1) % count) for i in range(ends)])  41.7 us
    dot_general x4, matrix products, coefficient(): jnp.einsum('bfv,bv->bf', features, field, precision=lax.Precision.HIGHEST)  22 us
    ppermute x7, starting transfers between devices, around_the_ring(): pieces = [lax.ppermute(pieces[0], axis, right), *pieces]  12.9 us
    ppermute x7, waiting for transfers between devices, around_the_ring(): pieces = [lax.ppermute(pieces[0], axis, right), *pieces]  12.5 us
  transfers between devices with their start and end apart: 35, of which 21 were waited for; matrix products, arithmetic and copies ran while one was open for 0% of the time, Pallas kernels for 0%

profile of v1, /device:TPU:129, one launch (start us, length us, event | category | flops | bytes accessed | tf_op | source)
XLA Modules:
  0.0 573.4 jit_solution(7082600023786779808)
XLA Ops:
  0.7 5.8 %fusion.8 = f32[32,1,64]{2,1,0:T(1,128)S(1)} fusion(f32[32,64,512]{2,1,0:T(8,128)} %param.8, f32[32,512,1]{1,0,2:T(8,128)} %bitcast.92), kind=kOutput, calls=%fused_computation.25 | convolution fusion | flops 12582912 | bytes 4268032 | tf_op jit(solution)/shard_map/bfv,bv->bf/dot_general | solution.py:38
  6.5 3.9 collective-permute-start.1
  10.4 1.9 collective-permute-start
  12.7 5.6 collective-permute-done
  18.2 4.0 collective-permute-start.3
  22.3 3.1 collective-permute-start.2
  26.8 1.9 collective-permute-start.5
  28.7 3.4 collective-permute-start.4
  32.1 4.4 collective-permute-done.4
  36.5 2.1 collective-permute-start.7
  38.6 5.2 collective-permute-start.6
  43.8 1.1 collective-permute-done.6
  45.2 4.3 fusion.25
  50.2 74.5 %all-reduce = (f32[]{:T(128)}, f32[]{:T(128)}) all-reduce(f32[]{:T(128)} %get-tuple-element.4, f32[]{:T(128)} %get-tuple-element.3), channel_id=1, replica_groups=mesh['gx'=32,'gy'=8] {'gx','gy'}, use_global_device_ids=true, to_apply=%region_1.2 | all-reduce | flops 2 | bytes 16 | tf_op jit(solution)/shard_map/psum | solution.py:42
  126.7 73.5 %psum.44 = f32[]{:T(128)} all-reduce(f32[]{:T(128)} %get-tuple-element.9), channel_id=1, replica_groups=mesh['gx'=32,'gy'=8] {'gx','gy'}, use_global_device_ids=true, to_apply=%region_6.7 | all-reduce | flops 1 | bytes 8 | tf_op jit(solution)/shard_map/psum | solution.py:42
  201.5 5.4 fusion.6
  206.9 3.8 collective-permute-start.9
  210.8 1.9 collective-permute-start.8
  212.7 5.9 %collective-permute-done.8 = f32[1,1,32,64]{3,2,1,0:T(8,128)S(1)} collective-permute-done((f32[1,1,32,64]{3,2,1,0:T(8,128)S(1)}, f32[1,1,32,64]{3,2,1,0:T(8,128)S(1)}, u32[]{:S(2)}, u32[]{:S(2)}) %collective-permute-start.8) | collective-permute-done | bytes 8224 | tf_op jit(solution)/shard_map/ppermute | solution.py:28
  218.6 4.0 collective-permute-start.11
  222.6 1.9 collective-permute-start.10
  224.5 1.2 collective-permute-done.10
  226.0 1.9 collective-permute-start.13
  227.9 3.4 collective-permute-start.12
  231.3 4.4 collective-permute-done.12
  235.7 3.2 collective-permute-start.15
  238.9 4.3 collective-permute-start.14
  243.2 1.0 collective-permute-done.14
  244.4 2.1 fusion.27
  247.1 73.2 %psum.45 = f32[]{:T(128)} all-reduce(f32[]{:T(128)} %multiply_reduce_fusion.2), channel_id=1, replica_groups=mesh['gx'=32,'gy'=8] {'gx','gy'}, use_global_device_ids=true, to_apply=%region_8.9 | all-reduce | flops 1 | bytes 8 | tf_op jit(solution)/shard_map/psum | solution.py:85
  322.3 73.3 %psum.46 = f32[]{:T(128)} all-reduce(f32[]{:T(128)} %get-tuple-element.7), channel_id=1, replica_groups=mesh['gx'=32,'gy'=8] {'gx','gy'}, use_global_device_ids=true, to_apply=%region_10.11 | all-reduce | flops 1 | bytes 8 | tf_op jit(solution)/shard_map/psum | solution.py:42
  397.0 5.4 fusion.4
  402.4 4.2 collective-permute-start.17
  406.6 1.9 collective-permute-start.16
  408.6 5.9 %collective-permute-done.16 = f32[1,1,32,64]{3,2,1,0:T(8,128)S(1)} collective-permute-done((f32[1,1,32,64]{3,2,1,0:T(8,128)S(1)}, f32[1,1,32,64]{3,2,1,0:T(8,128)S(1)}, u32[]{:S(2)}, u32[]{:S(2)}) %collective-permute-start.16) | collective-permute-done | bytes 8224 | tf_op jit(solution)/shard_map/ppermute | solution.py:28
  414.5 4.0 collective-permute-start.19
  418.5 1.9 collective-permute-start.18
  420.4 1.2 collective-permute-done.18
  421.8 1.9 collective-permute-start.21
  423.7 3.4 collective-permute-start.20
  427.1 4.4 collective-permute-done.20
  431.6 3.2 collective-permute-start.23
  434.8 4.1 collective-permute-start.22
  438.9 1.1 collective-permute-done.22
  440.3 2.1 fusion.29
  443.0 73.2 %psum.47 = f32[]{:T(128)} all-reduce(f32[]{:T(128)} %multiply_reduce_fusion), channel_id=1, replica_groups=mesh['gx'=32,'gy'=8] {'gx','gy'}, use_global_device_ids=true, to_apply=%region_12.13 | all-reduce | flops 1 | bytes 8 | tf_op jit(solution)/shard_map/psum | solution.py:85
  518.2 5.3 fusion.2
  523.5 3.7 collective-permute-start.25
  527.2 1.9 collective-permute-start.24
  529.1 5.9 %collective-permute-done.24 = f32[1,1,32,64]{3,2,1,0:T(8,128)S(1)} collective-permute-done((f32[1,1,32,64]{3,2,1,0:T(8,128)S(1)}, f32[1,1,32,64]{3,2,1,0:T(8,128)S(1)}, u32[]{:S(2)}, u32[]{:S(2)}) %collective-permute-start.24) | collective-permute-done | bytes 8224 | tf_op jit(solution)/shard_map/ppermute | solution.py:28
  535.0 4.0 collective-permute-start.27
  539.0 3.4 collective-permute-start.26
  542.5 1.1 collective-permute-done.26
  543.8 2.3 collective-permute-start.28
  547.1 2.3 collective-permute-start.29
  550.2 2.3 collective-permute-start.30
  553.4 2.3 collective-permute-start.31
  556.6 2.3 collective-permute-start.32
  558.9 1.9 collective-permute-done.32
  560.7 1.3 collective-permute-start.33
  562.0 3.1 collective-permute-done.33
  565.4 4.1 collective-permute-done.34
  569.6 2.8 gather_fusion
  572.5 1.0 fusion.1
  (90 shorter events, 10.8 us)
Async XLA Ops:
  0.6 11.7 %copy-start.6 = (s32[32,27]{1,0:T(8,128)S(1)}, s32[32,27]{1,0:T(8,128)}, u32[]{:S(2)}) copy-start(s32[32,27]{1,0:T(8,128)} %param.9) | copy-start | bytes 10372
  0.6 48.9 %copy-start.2 = (f32[32,512]{1,0:T(8,128)S(1)}, f32[32,512]{1,0:T(8,128)}, u32[]{:S(2)}) copy-start(f32[32,512]{1,0:T(8,128)} %param.7) | copy-start | bytes 196612
  0.7 48.9 %copy-start.3 = (f32[32,512]{1,0:T(8,128)S(1)}, f32[32,512]{1,0:T(8,128)}, u32[]{:S(2)}) copy-start(f32[32,512]{1,0:T(8,128)} %param.6) | copy-start | bytes 196612
  6.5 6.2 %collective-permute-start.1 = (f32[1,1,32,64]{3,2,1,0:T(8,128)S(1)}, f32[1,1,32,64]{3,2,1,0:T(8,128)S(1)}, u32[]{:S(2)}, u32[]{:S(2)}) collective-permute-start(f32[1,1,32,64]{3,2,1,0:T(8,128)S(1)} %bitcast.101), channel_id=1, source_target_pairs={{8,0},{16,8},{24,16},{32,24},{40,32},{48,40},{56,48},{64,56},{72,6... | collective-permute-start | bytes 24584 | tf_op jit(solution)/shard_map/ppermute | solution.py:30
  10.4 7.8 %collective-permute-start = (f32[1,1,32,64]{3,2,1,0:T(8,128)S(1)}, f32[1,1,32,64]{3,2,1,0:T(8,128)S(1)}, u32[]{:S(2)}, u32[]{:S(2)}) collective-permute-start(f32[1,1,32,64]{3,2,1,0:T(8,128)S(1)} %bitcast.102), channel_id=1, source_target_pairs={{0,8},{8,16},{16,24},{24,32},{32,40},{40,48},{48,56},{56,64},{64,7... | collective-permute-start | bytes 24584 | tf_op jit(solution)/shard_map/ppermute | solution.py:28
  18.2 7.4 %collective-permute-start.3 = (f32[3,1,32,64]{3,2,1,0:T(8,128)S(1)}, f32[3,1,32,64]{3,2,1,0:T(8,128)S(1)}, u32[]{:S(2)}, u32[]{:S(2)}) collective-permute-start(f32[3,1,32,64]{3,2,1,0:T(8,128)S(1)} %pad_maximum_fusion.7), channel_id=1, source_target_pairs={{1,0},{2,1},{3,2},{4,3},{5,4},{6,5},{7,6},{9,8},{10,9},{11,10},{12... | collective-permute-start | bytes 73736 | tf_op jit(solution)/shard_map/ppermute | solution.py:30
  22.3 4.3 collective-permute-start.2
  26.8 5.3 collective-permute-start.5
  28.7 7.8 %collective-permute-start.4 = (f32[1,1,32,64]{3,2,1,0:T(8,128)S(1)}, f32[1,1,32,64]{3,2,1,0:T(8,128)S(1)}, u32[]{:S(2)}, u32[]{:S(2)}) collective-permute-start(f32[1,1,32,64]{3,2,1,0:T(8,128)S(1)} %convolution_bitcast_fusion.2), channel_id=1, source_target_pairs={{0,8},{8,16},{16,24},{24,32},{32,40},{40,48},{48,56},{56,64},{64,7... | collective-permute-start | bytes 24584 | tf_op jit(solution)/shard_map/ppermute | solution.py:28
  36.5 7.3 %collective-permute-start.7 = (f32[3,1,32,64]{3,2,1,0:T(8,128)S(1)}, f32[3,1,32,64]{3,2,1,0:T(8,128)S(1)}, u32[]{:S(2)}, u32[]{:S(2)}) collective-permute-start(f32[3,1,32,64]{3,2,1,0:T(8,128)S(1)} %pad_maximum_fusion.8), channel_id=1, source_target_pairs={{1,0},{2,1},{3,2},{4,3},{5,4},{6,5},{7,6},{9,8},{10,9},{11,10},{12... | collective-permute-start | bytes 73736 | tf_op jit(solution)/shard_map/ppermute | solution.py:30
  38.6 6.4 %collective-permute-start.6 = (f32[3,1,32,64]{3,2,1,0:T(8,128)S(1)}, f32[3,1,32,64]{3,2,1,0:T(8,128)S(1)}, u32[]{:S(2)}, u32[]{:S(2)}) collective-permute-start(f32[3,1,32,64]{3,2,1,0:T(8,128)S(1)} %pad_maximum_fusion.8), channel_id=1, source_target_pairs={{0,1},{1,2},{2,3},{3,4},{4,5},{5,6},{6,7},{8,9},{9,10},{10,11},{11... | collective-permute-start | bytes 73736 | tf_op jit(solution)/shard_map/ppermute | solution.py:28
  201.5 42.9 %copy-start = (f32[32,64,512]{2,1,0:T(8,128)S(1)}, f32[32,64,512]{2,1,0:T(8,128)}, u32[]{:S(2)}) copy-start(f32[32,64,512]{2,1,0:T(8,128)} %param.8) | copy-start | bytes 12582916
  206.9 5.8 %collective-permute-start.9 = (f32[1,1,32,64]{3,2,1,0:T(8,128)S(1)}, f32[1,1,32,64]{3,2,1,0:T(8,128)S(1)}, u32[]{:S(2)}, u32[]{:S(2)}) collective-permute-start(f32[1,1,32,64]{3,2,1,0:T(8,128)S(1)} %bitcast.109), channel_id=1, source_target_pairs={{8,0},{16,8},{24,16},{32,24},{40,32},{48,40},{56,48},{64,56},{72,6... | collective-permute-start | bytes 24584 | tf_op jit(solution)/shard_map/ppermute | solution.py:30
  210.8 7.8 %collective-permute-start.8 = (f32[1,1,32,64]{3,2,1,0:T(8,128)S(1)}, f32[1,1,32,64]{3,2,1,0:T(8,128)S(1)}, u32[]{:S(2)}, u32[]{:S(2)}) collective-permute-start(f32[1,1,32,64]{3,2,1,0:T(8,128)S(1)} %bitcast.110), channel_id=1, source_target_pairs={{0,8},{8,16},{16,24},{24,32},{32,40},{40,48},{48,56},{56,64},{64,7... | collective-permute-start | bytes 24584 | tf_op jit(solution)/shard_map/ppermute | solution.py:28
  218.6 5.9 %collective-permute-start.11 = (f32[3,1,32,64]{3,2,1,0:T(8,128)S(1)}, f32[3,1,32,64]{3,2,1,0:T(8,128)S(1)}, u32[]{:S(2)}, u32[]{:S(2)}) collective-permute-start(f32[3,1,32,64]{3,2,1,0:T(8,128)S(1)} %pad_maximum_fusion.9), channel_id=1, source_target_pairs={{1,0},{2,1},{3,2},{4,3},{5,4},{6,5},{7,6},{9,8},{10,9},{11,10},{12... | collective-permute-start | bytes 73736 | tf_op jit(solution)/shard_map/ppermute | solution.py:30
  222.6 3.1 collective-permute-start.10
  226.0 5.3 collective-permute-start.13
  227.9 7.8 %collective-permute-start.12 = (f32[1,1,32,64]{3,2,1,0:T(8,128)S(1)}, f32[1,1,32,64]{3,2,1,0:T(8,128)S(1)}, u32[]{:S(2)}, u32[]{:S(2)}) collective-permute-start(f32[1,1,32,64]{3,2,1,0:T(8,128)S(1)} %convolution_bitcast_fusion.1), channel_id=1, source_target_pairs={{0,8},{8,16},{16,24},{24,32},{32,40},{40,48},{48,56},{56,64},{64,7... | collective-permute-start | bytes 24584 | tf_op jit(solution)/shard_map/ppermute | solution.py:28
  235.7 7.5 %collective-permute-start.15 = (f32[3,1,32,64]{3,2,1,0:T(8,128)S(1)}, f32[3,1,32,64]{3,2,1,0:T(8,128)S(1)}, u32[]{:S(2)}, u32[]{:S(2)}) collective-permute-start(f32[3,1,32,64]{3,2,1,0:T(8,128)S(1)} %pad_maximum_fusion.10), channel_id=1, source_target_pairs={{1,0},{2,1},{3,2},{4,3},{5,4},{6,5},{7,6},{9,8},{10,9},{11,10},{12... | collective-permute-start | bytes 73736 | tf_op jit(solution)/shard_map/ppermute | solution.py:30
  238.9 5.2 collective-permute-start.14
  396.9 43.3 %copy-start.1 = (f32[32,64,512]{2,1,0:T(8,128)S(1)}, f32[32,64,512]{2,1,0:T(8,128)}, u32[]{:S(2)}) copy-start(f32[32,64,512]{2,1,0:T(8,128)} %param.8) | copy-start | bytes 12582916
  402.4 6.2 %collective-permute-start.17 = (f32[1,1,32,64]{3,2,1,0:T(8,128)S(1)}, f32[1,1,32,64]{3,2,1,0:T(8,128)S(1)}, u32[]{:S(2)}, u32[]{:S(2)}) collective-permute-start(f32[1,1,32,64]{3,2,1,0:T(8,128)S(1)} %bitcast.105), channel_id=1, source_target_pairs={{8,0},{16,8},{24,16},{32,24},{40,32},{48,40},{56,48},{64,56},{72,6... | collective-permute-start | bytes 24584 | tf_op jit(solution)/shard_map/ppermute | solution.py:30
  406.6 7.8 %collective-permute-start.16 = (f32[1,1,32,64]{3,2,1,0:T(8,128)S(1)}, f32[1,1,32,64]{3,2,1,0:T(8,128)S(1)}, u32[]{:S(2)}, u32[]{:S(2)}) collective-permute-start(f32[1,1,32,64]{3,2,1,0:T(8,128)S(1)} %bitcast.106), channel_id=1, source_target_pairs={{0,8},{8,16},{16,24},{24,32},{32,40},{40,48},{48,56},{56,64},{64,7... | collective-permute-start | bytes 24584 | tf_op jit(solution)/shard_map/ppermute | solution.py:28
  414.5 5.9 %collective-permute-start.19 = (f32[3,1,32,64]{3,2,1,0:T(8,128)S(1)}, f32[3,1,32,64]{3,2,1,0:T(8,128)S(1)}, u32[]{:S(2)}, u32[]{:S(2)}) collective-permute-start(f32[3,1,32,64]{3,2,1,0:T(8,128)S(1)} %pad_maximum_fusion.11), channel_id=1, source_target_pairs={{1,0},{2,1},{3,2},{4,3},{5,4},{6,5},{7,6},{9,8},{10,9},{11,10},{12... | collective-permute-start | bytes 73736 | tf_op jit(solution)/shard_map/ppermute | solution.py:30
  418.5 3.1 collective-permute-start.18
  421.8 5.3 collective-permute-start.21
  423.7 7.8 %collective-permute-start.20 = (f32[1,1,32,64]{3,2,1,0:T(8,128)S(1)}, f32[1,1,32,64]{3,2,1,0:T(8,128)S(1)}, u32[]{:S(2)}, u32[]{:S(2)}) collective-permute-start(f32[1,1,32,64]{3,2,1,0:T(8,128)S(1)} %convolution_bitcast_fusion), channel_id=1, source_target_pairs={{0,8},{8,16},{16,24},{24,32},{32,40},{40,48},{48,56},{56,64},{64,7... | collective-permute-start | bytes 24584 | tf_op jit(solution)/shard_map/ppermute | solution.py:28
  431.6 7.3 %collective-permute-start.23 = (f32[3,1,32,64]{3,2,1,0:T(8,128)S(1)}, f32[3,1,32,64]{3,2,1,0:T(8,128)S(1)}, u32[]{:S(2)}, u32[]{:S(2)}) collective-permute-start(f32[3,1,32,64]{3,2,1,0:T(8,128)S(1)} %pad_maximum_fusion.12), channel_id=1, source_target_pairs={{1,0},{2,1},{3,2},{4,3},{5,4},{6,5},{7,6},{9,8},{10,9},{11,10},{12... | collective-permute-start | bytes 73736 | tf_op jit(solution)/shard_map/ppermute | solution.py:30
  434.8 5.2 collective-permute-start.22
  440.2 121.8 %copy-start.7 = (s32[1024]{0:T(1024)S(1)}, s32[1024]{0:T(1024)}, u32[]{:S(2)}) copy-start(s32[1024]{0:T(1024)} %param.11) | copy-start | bytes 12292
  440.3 124.9 %copy-start.5 = (f32[64,1024]{1,0:T(8,128)S(1)}, f32[64,1024]{1,0:T(8,128)}, u32[]{:S(2)}) copy-start(f32[64,1024]{1,0:T(8,128)} %param.10) | copy-start | bytes 786436
  518.2 54.3 %copy-start.4 = (f32[32,512]{1,0:T(8,128)}, f32[32,512]{1,0:T(8,128)S(1)}, u32[]{:S(2)}) copy-start(f32[32,512]{1,0:T(8,128)S(1)} %get-tuple-element.12) | copy-start | bytes 196612
  523.5 5.6 collective-permute-start.25
  527.2 7.8 %collective-permute-start.24 = (f32[1,1,32,64]{3,2,1,0:T(8,128)S(1)}, f32[1,1,32,64]{3,2,1,0:T(8,128)S(1)}, u32[]{:S(2)}, u32[]{:S(2)}) collective-permute-start(f32[1,1,32,64]{3,2,1,0:T(8,128)S(1)} %bitcast.114), channel_id=1, source_target_pairs={{0,8},{8,16},{16,24},{24,32},{32,40},{40,48},{48,56},{56,64},{64,7... | collective-permute-start | bytes 24584 | tf_op jit(solution)/shard_map/ppermute | solution.py:28
  535.0 7.5 %collective-permute-start.27 = (f32[3,1,32,64]{3,2,1,0:T(8,128)S(1)}, f32[3,1,32,64]{3,2,1,0:T(8,128)S(1)}, u32[]{:S(2)}, u32[]{:S(2)}) collective-permute-start(f32[3,1,32,64]{3,2,1,0:T(8,128)S(1)} %pad_maximum_fusion.13), channel_id=1, source_target_pairs={{1,0},{2,1},{3,2},{4,3},{5,4},{6,5},{7,6},{9,8},{10,9},{11,10},{12... | collective-permute-start | bytes 73736 | tf_op jit(solution)/shard_map/ppermute | solution.py:30
  539.0 4.6 collective-permute-start.26
  543.8 3.2 collective-permute-start.28
  547.1 3.2 collective-permute-start.29
  550.2 3.2 collective-permute-start.30
  553.4 3.2 collective-permute-start.31
  556.6 4.2 collective-permute-start.32
  560.7 4.4 collective-permute-start.33
  565.1 4.4 collective-permute-start.34
